TPU v7x, 32 devices: a whole 2x2x4 slice. The times are simulated.
32 devices in a mesh: groups: 2 (over x), seq: 8 (over z, y), inner: 2 (over core).
Axes of the slice: x: 2, y: 2, z: 4, core: 2. Of those that a mesh axis runs over, the one named last changes fastest.
Arguments:
- queries: bfloat16 [8192, 2048], P(('groups', 'seq', 'inner')), parts along dimension 0, may hold values from -6 to 6
- key_vectors: bfloat16 [8192, 2048], P(('groups', 'seq', 'inner')), parts along dimension 0, may hold values from -6 to 6
- value_vectors: bfloat16 [8192, 2048], P(('groups', 'seq', 'inner')), parts along dimension 0, may hold values from -6 to 6
- cache_state: float32 [8, 16, 128, 128], P('groups', 'inner'), parts along dimension 0, may hold values from -0.375 to 0.375
- prefix_lengths: int32 [8], P('groups'), parts along dimension 0, may hold values from 0 to 1024
- new_lengths: int32 [8], P('groups'), parts along dimension 0, may hold values from 1 to 3072, 4096 in all
- out_gain: float32 [2048], replicated, may hold values from 0.5 to 1.5
Outputs:
- attended: bfloat16 [8192, 2048], P(('groups', 'seq', 'inner')), parts along dimension 0
There are 2 independent parts, one for each index of `groups`. A program takes and returns all parts, laid end to end along the dimension named above; an argument that names none is the same for every part. Nothing has to cross between parts.
Inputs may be any that keep to these rules, and one draw needn't show every extreme that they name: `new_lengths`: every prompt has at least one new token and the largest has exactly 3072; the lengths sum to 4096.
All inputs are finite; a program needn't handle non-finite values.
Results may differ from a plain program's by a relative error of at most 0.0055.
Values sent between devices are 32-bit elements; how exact they have to be, the bound alone decides.
A program may use at most 128 MiB of HBM per device.

v0:
```python
import functools
import math
import jax
import jax.numpy as jnp
from jax import lax
from jax.experimental import pallas as pl
from jax.experimental.pallas import tpu as pltpu
from jax.sharding import PartitionSpec as P

H = 16
DK = 128
VMEM = pltpu.VMEM
MESH = pl.DeviceIdType.MESH


def features(entries):
    values_f = entries.astype(jnp.float32)
    return jnp.where(values_f > 0, values_f + 1.0, jnp.exp(jnp.minimum(values_f, 0.0))).astype(
        jnp.bfloat16
    )


def prompt_starts(lengths_ref, prompts):
    starts, total = [], jnp.int32(0)
    for p in range(prompts):
        starts.append(total)
        total = total + lengths_ref[p]
    return starts


def no_start(starts, low, high):
    clear = jnp.float32(1.0)
    for start in starts:
        clear = clear * jnp.where((start >= low) & (start < high), 0.0, 1.0)
    return clear


def layer_kernel(
    A, B, lengths_ref, prefix_ref, k_ref, v_ref, gain_ref, q_hbm, cache_hbm, out_ref,
    q_ref, near_ref, far_ref, key_ref, carry_query_ref, acc_ref, own_ref, carry_ref, mask_ref,
    prompt_mask_ref, carry_mask_ref,
    pair_buf, x_buf, row_buf, z_in, z_out, back_buf,
    pair_s, pair_r, row_s, row_r, z_s, z_r, back_s, back_r, far_s, far_r, near_sem, q_sem,
):
    half = pair_buf.shape[0]
    rows = k_ref.shape[0]
    prompts = near_ref.shape[0]
    s = lax.axis_index("seq")
    c = lax.axis_index("inner")
    other = 1 - c
    a, b = s // B, s % B
    first, last = a == 0, a == A - 1
    barrier = pltpu.get_barrier_semaphore()

    def greet(device):
        pl.semaphore_signal(barrier, inc=1, device_id=device, device_id_type=MESH)

    greet({"inner": other})
    mates = [a * B + (b + k) % B for k in range(1, B)]
    for mate in mates:
        greet({"seq": mate})
    pl.when(jnp.logical_not(first))(lambda: greet({"seq": s - B}))
    pl.when(jnp.logical_not(last))(lambda: greet({"seq": s + B}))

    def remote(src, dst, send, recv, device):
        return pltpu.make_async_remote_copy(
            src_ref=src, dst_ref=dst, send_sem=send, recv_sem=recv,
            device_id=device, device_id_type=MESH,
        )

    def pair(h):
        return remote(
            own_ref.at[other * half + h], pair_buf.at[h], pair_s.at[h], pair_r.at[h],
            {"inner": other},
        )

    def row(h):
        return [
            remote(x_buf.at[h], row_buf.at[k, h], row_s.at[k, h], row_r.at[k, h], {"seq": mates[k]})
            for k in range(B - 1)
        ]

    def down(h):
        return remote(
            z_out.at[h], z_in.at[h], z_s.at[h], z_r.at[h], {"seq": jnp.minimum(s + B, A * B - 1)}
        )

    def back(h):
        return remote(
            back_buf.at[h], carry_ref.at[c * half + h], back_s.at[h], back_r.at[h],
            {"inner": other},
        )

    near_copy = pltpu.make_async_copy(cache_hbm, near_ref, near_sem)
    q_copy = pltpu.make_async_copy(q_hbm, q_ref, q_sem)
    far_copy = remote(cache_hbm, far_ref, far_s, far_r, {"inner": other})
    q_copy.start()
    near_copy.start()

    starts = prompt_starts(lengths_ref, prompts)
    pair_rows = 2 * rows
    here = s * pair_rows
    first_row = here + c * rows
    row_begin, row_end = a * B * pair_rows, (a + 1) * B * pair_rows
    is_zero = jnp.where(c == 0, 1.0, 0.0).astype(jnp.float32)
    is_one = 1.0 - is_zero
    keep_zero = no_start(starts, here, here + rows)
    keep_one = no_start(starts, here + rows, here + pair_rows)
    mine_weight = is_one + is_zero * keep_one
    theirs_weight = is_zero + is_one * keep_one
    total_weights, prefix_weights = [], []
    for k in range(B):
        whose = (b + B - k) % B
        end = (a * B + whose + 1) * pair_rows
        total_weights.append(no_start(starts, end, row_end))
        prefix_weights.append(no_start(starts, end, here) * jnp.where(whose < b, 1.0, 0.0))
    keep_row = no_start(starts, row_begin, row_end)
    keep_prefix = no_start(starts, row_begin, here)

    last_start, first_start = jnp.int32(0), jnp.int32(0)
    for start in starts:
        last_start = jnp.maximum(last_start, jnp.where(start < first_row + rows, start, 0))
        first_start = jnp.maximum(first_start, jnp.where(start <= first_row, start, 0))
    column = lax.broadcasted_iota(jnp.int32, (rows, DK), 0) + first_row
    in_last = column >= last_start

    def columns(head):
        return pl.ds(pl.multiple_of(head * DK, DK), DK)

    def own_state(head):
        cols = columns(head)
        key_feat = features(k_ref[:, cols])
        key_ref[:, cols] = key_feat
        key_feat = jnp.where(in_last, key_feat, jnp.zeros_like(key_feat))
        own_ref[head] = lax.dot_general(
            key_feat, v_ref[:, cols], (((0,), (0,)), ((), ())), preferred_element_type=jnp.float32
        )

    ends = first.astype(jnp.int32) + last.astype(jnp.int32)
    pl.semaphore_wait(barrier, B + 2 - ends)

    @pl.loop(0, half)
    def _(h):
        own_state(other * half + h)
        pair(h).start()

    far_copy.start()

    @pl.loop(0, half)
    def _(h):
        own_state(c * half + h)
        pair(h).wait_recv()
        x_buf[h] = mine_weight * own_ref[c * half + h] + theirs_weight * pair_buf[h]
        for copy in row(h):
            copy.start()

    @pl.when(first)
    def _():
        z_in[...] = jnp.zeros_like(z_in)

    segment_down = lax.broadcasted_iota(jnp.int32, (rows, rows), 0) + first_row
    segment_along = lax.broadcasted_iota(jnp.int32, (rows, rows), 1) + first_row
    mask = segment_down >= segment_along
    for start in starts:
        mask = mask & ((segment_down < start) | (segment_along >= start))
    mask_ref[...] = jnp.where(mask, 1.0, 0.0)
    for p in range(prompts):
        inside = column >= starts[p]
        if p + 1 < prompts:
            inside = inside & (column < starts[p + 1])
        prompt_mask_ref[p] = jnp.where(inside, 1.0, 0.0).astype(jnp.bfloat16)
    after = jnp.int32(2**31 - 1)
    for start in starts:
        after = jnp.minimum(after, jnp.where(start > first_row, start, after))
    carried = (column < after) & (first_start < first_row)
    carry_mask_ref[...] = jnp.where(carried, 1.0, 0.0).astype(jnp.bfloat16)
    near_copy.wait()
    q_copy.wait()
    far_copy.wait()

    def split(state):
        upper = state.astype(jnp.bfloat16)
        return upper, (state - upper.astype(jnp.float32)).astype(jnp.bfloat16)

    def local_terms(cached, head, h):
        cols = columns(head)
        query_feat = features(q_ref[:, cols])
        carry_query_ref[:, cols] = query_feat * carry_mask_ref[...]
        scores = lax.dot_general(
            query_feat, key_ref[:, cols], (((1,), (1,)), ((), ())),
            preferred_element_type=jnp.float32,
        )
        scores = (scores * mask_ref[...]).astype(jnp.bfloat16)
        acc = jnp.dot(scores, v_ref[:, cols], preferred_element_type=jnp.float32)
        uppers, lowers, queries = [], [], []
        for p in range(prompts):
            upper, lower = split(prefix_ref[p].astype(jnp.float32) * cached[p, h])
            uppers.append(upper)
            lowers.append(lower)
            queries.append(query_feat * prompt_mask_ref[p])
        masked = jnp.concatenate(queries, axis=1)
        acc += jnp.dot(masked, jnp.concatenate(uppers, 0), preferred_element_type=jnp.float32)
        acc += jnp.dot(masked, jnp.concatenate(lowers, 0), preferred_element_type=jnp.float32)
        acc_ref[:, cols] = acc

    def both_local(h):
        local_terms(near_ref, c * half + h, h)
        local_terms(far_ref, other * half + h, h)

    def finish(head):
        cols = columns(head)
        query = carry_query_ref[:, cols]
        state = jnp.concatenate(split(carry_ref[head]), axis=0)
        mixed = acc_ref[:, cols] + jnp.dot(
            jnp.concatenate([query, query], axis=1), state, preferred_element_type=jnp.float32
        )
        scale = 1.0 / jnp.sqrt(jnp.mean(mixed * mixed, axis=1, keepdims=True) + 1e-06)
        out_ref[:, cols] = (mixed * scale * gain_ref[:, cols]).astype(jnp.bfloat16)

    def both_finish(h):
        back(h).wait_recv()
        finish(c * half + h)
        finish(other * half + h)

    ahead = (half * a) // max(A - 1, 1)

    @pl.loop(0, ahead)
    def _(h):
        both_local(h)

    late = a >= A // 2

    @pl.loop(0, half)
    def _(h):
        for copy in row(h):
            copy.wait_recv()
        total = total_weights[0] * x_buf[h]
        prefix = jnp.zeros_like(total)
        for k in range(1, B):
            got = row_buf[k - 1, h]
            total = total + total_weights[k] * got
            prefix = prefix + prefix_weights[k] * got
        pl.when(jnp.logical_not(first))(lambda: down(h).wait_recv())
        incoming = z_in[h]
        z_out[h] = total + keep_row * incoming
        pl.when(jnp.logical_not(last))(lambda: down(h).start())
        at_zero = prefix + keep_prefix * incoming
        mine, theirs = own_ref[c * half + h], pair_buf[h]
        at_one = is_zero * mine + is_one * theirs + keep_zero * at_zero
        back_buf[h] = is_one * at_zero + is_zero * at_one
        back(h).start()
        carry_ref[c * half + h] = is_zero * at_zero + is_one * at_one
        pl.when(h >= ahead)(lambda: both_local(h))
        pl.when(late & (h > 0))(lambda: both_finish(h - 1))

    @pl.loop(jnp.where(late, half - 1, 0), half)
    def _(h):
        both_finish(h)

    @pl.loop(0, half)
    def _(h):
        pair(h).wait_send()
        for copy in row(h):
            copy.wait_send()
        pl.when(jnp.logical_not(last))(lambda: down(h).wait_send())
        back(h).wait_send()


def on_device(
    count, queries, key_vectors, value_vectors, cache_state, prefix_lengths, new_lengths, out_gain
):
    rows, width = queries.shape
    prompts, half = cache_state.shape[:2]
    vmem = pl.BlockSpec(memory_space=VMEM)
    smem = pl.BlockSpec(memory_space=pltpu.SMEM)
    anywhere = pl.BlockSpec(memory_space=pl.ANY)
    B = max(d for d in range(1, math.isqrt(count) + 1) if count % d == 0)
    A = count // B
    f32, bf16 = jnp.float32, jnp.bfloat16
    part = VMEM((half, DK, DK), f32)
    whole = VMEM((2 * half, DK, DK), f32)
    cache = VMEM(cache_state.shape, f32)
    sems = lambda *shape: pltpu.SemaphoreType.DMA(shape)
    return pl.pallas_call(
        functools.partial(layer_kernel, A, B),
        out_shape=jax.ShapeDtypeStruct((rows, width), bf16),
        in_specs=[smem, smem, vmem, vmem, vmem, anywhere, anywhere],
        out_specs=vmem,
        scratch_shapes=[
            VMEM((rows, width), bf16), cache, cache, VMEM((rows, width), bf16),
            VMEM((rows, width), bf16), VMEM((rows, width), f32), whole, whole,
            VMEM((rows, rows), f32), VMEM((prompts, rows, DK), bf16), VMEM((rows, DK), bf16),
            part, part, VMEM((B - 1, half, DK, DK), f32), part, part, part,
            sems(half), sems(half), sems(B - 1, half), sems(B - 1, half),
            sems(half), sems(half), sems(half), sems(half),
            pltpu.SemaphoreType.DMA, pltpu.SemaphoreType.DMA,
            pltpu.SemaphoreType.DMA, pltpu.SemaphoreType.DMA,
        ],
        compiler_params=pltpu.CompilerParams(collective_id=0, has_side_effects=True),
        name="layer",
    )(
        new_lengths, prefix_lengths, key_vectors, value_vectors, out_gain[None, :],
        queries, cache_state,
    )


def solution(mesh):
    in_specs = (
        P(("groups", "seq", "inner"), None),
        P(("groups", "seq", "inner"), None),
        P(("groups", "seq", "inner"), None),
        P("groups", "inner", None, None),
        P("groups"),
        P("groups"),
        P(),
    )
    out_specs = P(("groups", "seq", "inner"), None)
    return jax.shard_map(
        functools.partial(on_device, mesh.shape["seq"]),
        mesh=mesh, in_specs=in_specs, out_specs=out_specs, check_vma=False,
    )
```

profile of v0, /device:TPU:29, one launch (start us, length us, event | category | flops | bytes accessed | tf_op | source)
XLA Modules:
  0.0 33.9 jit_solution(9809080384923362491)
XLA Ops:
  0.0 31.6 %layer.1 = bf16[256,2048]{1,0:T(8,128)(2,1)} custom-call(s32[4]{0:T(128)} %lengths_ref.1, s32[4]{0:T(128)} %prefix_ref.1, bf16[256,2048]{1,0:T(8,128)(2,1)} %k_ref.1, bf16[256,2048]{1,0:T(8,128)(2,1)} %v_ref.1, f32[1,2048]{1,0:T(1,128)} %bitcast.1, bf16[256,2048]{1,0:T(8,128)(2,1)} %q_hbm.1, f32[4,8,128,128]{3,2,1,0:T(8,128)} %cache_hbm.1), custom_call_target="tpu_custom_call" | custom-call | tf_op jit(solution)/shard_map/layer/pallas_call | solution.py:284
  31.6 2.3 %copy.9 = bf16[256,2048]{1,0:T(8,128)(2,1)} copy(bf16[256,2048]{1,0:T(8,128)(2,1)} %layer.1) | data formatting | bytes 2097152
where the time goes:
time: 34.5 us; the launch traced here: 33.9 us
  Pallas kernels  31.6 us (92%)
  local copies, waits for them, and re-layouts  2.3 us (7%)
    pallas_call x1, Pallas kernels, on_device(): pl.pallas_call(functools.partial(layer_kernel, A, B), out_shape=jax.Shape...  31.6 us
    unnamed x1, local copies, waits for them, and re-layouts  2.3 us

commit v1 on v0

--- a/solution.py
+++ b/solution.py
@@ -37,14 +37,16 @@
 
 def layer_kernel(
     A, B, lengths_ref, prefix_ref, k_ref, v_ref, gain_ref, q_hbm, cache_hbm, out_ref,
-    q_ref, near_ref, far_ref, key_ref, carry_query_ref, acc_ref, own_ref, carry_ref, mask_ref,
+    q_ref, cached_ref, key_ref, carry_query_ref, acc_ref, own_ref, carry_ref, mask_ref,
     prompt_mask_ref, carry_mask_ref,
     pair_buf, x_buf, row_buf, z_in, z_out, back_buf,
     pair_s, pair_r, row_s, row_r, z_s, z_r, back_s, back_r, far_s, far_r, near_sem, q_sem,
 ):
     half = pair_buf.shape[0]
     rows = k_ref.shape[0]
-    prompts = near_ref.shape[0]
+    prompts = cached_ref.shape[1]
+    chunk_rows = DK // 2
+    chunks = 2 * half
     s = lax.axis_index("seq")
     c = lax.axis_index("inner")
     other = 1 - c
@@ -74,26 +76,36 @@
             {"inner": other},
         )
 
-    def row(h):
+    def piece(ref, head, u):
+        return ref.at[head, pl.ds(pl.multiple_of(u * chunk_rows, chunk_rows), chunk_rows)]
+
+    def row(h, u):
+        j = 2 * h + u
         return [
-            remote(x_buf.at[h], row_buf.at[k, h], row_s.at[k, h], row_r.at[k, h], {"seq": mates[k]})
+            remote(
+                piece(x_buf, h, u), piece(row_buf.at[k], h, u), row_s.at[k, j], row_r.at[k, j],
+                {"seq": mates[k]},
+            )
             for k in range(B - 1)
         ]
 
-    def down(h):
+    def down(h, u):
+        j = 2 * h + u
         return remote(
-            z_out.at[h], z_in.at[h], z_s.at[h], z_r.at[h], {"seq": jnp.minimum(s + B, A * B - 1)}
-        )
-
-    def back(h):
+            piece(z_out, h, u), piece(z_in, h, u), z_s.at[j], z_r.at[j],
+            {"seq": jnp.minimum(s + B, A * B - 1)},
+        )
+
+    def back(h, u):
+        j = 2 * h + u
         return remote(
-            back_buf.at[h], carry_ref.at[c * half + h], back_s.at[h], back_r.at[h],
+            piece(back_buf, h, u), piece(carry_ref, c * half + h, u), back_s.at[j], back_r.at[j],
             {"inner": other},
         )
 
-    near_copy = pltpu.make_async_copy(cache_hbm, near_ref, near_sem)
+    near_copy = pltpu.make_async_copy(cache_hbm, cached_ref.at[0], near_sem)
     q_copy = pltpu.make_async_copy(q_hbm, q_ref, q_sem)
-    far_copy = remote(cache_hbm, far_ref, far_s, far_r, {"inner": other})
+    far_copy = remote(cache_hbm, cached_ref.at[1], far_s, far_r, {"inner": other})
     q_copy.start()
     near_copy.start()
 
@@ -136,23 +148,28 @@
             key_feat, v_ref[:, cols], (((0,), (0,)), ((), ())), preferred_element_type=jnp.float32
         )
 
+    def spread(h):
+        pair(h).wait_recv()
+        x_buf[h] = mine_weight * own_ref[c * half + h] + theirs_weight * pair_buf[h]
+        for u in range(2):
+            for copy in row(h, u):
+                copy.start()
+
+    own_state(other * half)
     ends = first.astype(jnp.int32) + last.astype(jnp.int32)
     pl.semaphore_wait(barrier, B + 2 - ends)
-
-    @pl.loop(0, half)
+    pair(0).start()
+    own_state(c * half)
+
+    @pl.loop(1, half)
     def _(h):
         own_state(other * half + h)
         pair(h).start()
+        own_state(c * half + h)
+        spread(h - 1)
 
     far_copy.start()
-
-    @pl.loop(0, half)
-    def _(h):
-        own_state(c * half + h)
-        pair(h).wait_recv()
-        x_buf[h] = mine_weight * own_ref[c * half + h] + theirs_weight * pair_buf[h]
-        for copy in row(h):
-            copy.start()
+    spread(half - 1)
 
     @pl.when(first)
     def _():
@@ -182,7 +199,8 @@
         upper = state.astype(jnp.bfloat16)
         return upper, (state - upper.astype(jnp.float32)).astype(jnp.bfloat16)
 
-    def local_terms(cached, head, h):
+    def local_terms(h, side):
+        head = jnp.where(side == 0, c, other) * half + h
         cols = columns(head)
         query_feat = features(q_ref[:, cols])
         carry_query_ref[:, cols] = query_feat * carry_mask_ref[...]
@@ -194,7 +212,7 @@
         acc = jnp.dot(scores, v_ref[:, cols], preferred_element_type=jnp.float32)
         uppers, lowers, queries = [], [], []
         for p in range(prompts):
-            upper, lower = split(prefix_ref[p].astype(jnp.float32) * cached[p, h])
+            upper, lower = split(prefix_ref[p].astype(jnp.float32) * cached_ref[side, p, h])
             uppers.append(upper)
             lowers.append(lower)
             queries.append(query_feat * prompt_mask_ref[p])
@@ -203,10 +221,6 @@
         acc += jnp.dot(masked, jnp.concatenate(lowers, 0), preferred_element_type=jnp.float32)
         acc_ref[:, cols] = acc
 
-    def both_local(h):
-        local_terms(near_ref, c * half + h, h)
-        local_terms(far_ref, other * half + h, h)
-
     def finish(head):
         cols = columns(head)
         query = carry_query_ref[:, cols]
@@ -217,53 +231,65 @@
         scale = 1.0 / jnp.sqrt(jnp.mean(mixed * mixed, axis=1, keepdims=True) + 1e-06)
         out_ref[:, cols] = (mixed * scale * gain_ref[:, cols]).astype(jnp.bfloat16)
 
-    def both_finish(h):
-        back(h).wait_recv()
-        finish(c * half + h)
-        finish(other * half + h)
-
-    ahead = (half * a) // max(A - 1, 1)
-
-    @pl.loop(0, ahead)
-    def _(h):
-        both_local(h)
-
+    def unit(i):
+        @pl.when(i < chunks)
+        def _():
+            local_terms(i // 2, i % 2)
+
+        @pl.when(i >= chunks)
+        def _():
+            h, side = (i - chunks) // 2, i % 2
+
+            @pl.when(side == 0)
+            def _():
+                back(h, 0).wait_recv()
+                back(h, 1).wait_recv()
+
+            finish(jnp.where(side == 0, c, other) * half + h)
+
+    ahead = (chunks * a) // max(A - 1, 1)
     late = a >= A // 2
 
-    @pl.loop(0, half)
-    def _(h):
-        for copy in row(h):
+    def done(j):
+        full = jnp.maximum(ahead, jnp.minimum(ahead + j, chunks + j - 4))
+        return jnp.where(late, full, ahead + j // 2)
+
+    pl.loop(0, ahead)(unit)
+
+    @pl.loop(0, chunks)
+    def _(j):
+        h, u = j // 2, j % 2
+        part = pl.ds(pl.multiple_of(u * chunk_rows, chunk_rows), chunk_rows)
+        for copy in row(h, u):
             copy.wait_recv()
-        total = total_weights[0] * x_buf[h]
+        total = total_weights[0] * x_buf[h, part]
         prefix = jnp.zeros_like(total)
         for k in range(1, B):
-            got = row_buf[k - 1, h]
+            got = row_buf[k - 1, h, part]
             total = total + total_weights[k] * got
             prefix = prefix + prefix_weights[k] * got
-        pl.when(jnp.logical_not(first))(lambda: down(h).wait_recv())
-        incoming = z_in[h]
-        z_out[h] = total + keep_row * incoming
-        pl.when(jnp.logical_not(last))(lambda: down(h).start())
+        pl.when(jnp.logical_not(first))(lambda: down(h, u).wait_recv())
+        incoming = z_in[h, part]
+        z_out[h, part] = total + keep_row * incoming
+        pl.when(jnp.logical_not(last))(lambda: down(h, u).start())
         at_zero = prefix + keep_prefix * incoming
-        mine, theirs = own_ref[c * half + h], pair_buf[h]
+        mine, theirs = own_ref[c * half + h, part], pair_buf[h, part]
         at_one = is_zero * mine + is_one * theirs + keep_zero * at_zero
-        back_buf[h] = is_one * at_zero + is_zero * at_one
-        back(h).start()
-        carry_ref[c * half + h] = is_zero * at_zero + is_one * at_one
-        pl.when(h >= ahead)(lambda: both_local(h))
-        pl.when(late & (h > 0))(lambda: both_finish(h - 1))
-
-    @pl.loop(jnp.where(late, half - 1, 0), half)
-    def _(h):
-        both_finish(h)
+        back_buf[h, part] = is_one * at_zero + is_zero * at_one
+        back(h, u).start()
+        carry_ref[c * half + h, part] = is_zero * at_zero + is_one * at_one
+        pl.loop(done(j), done(j + 1))(unit)
+
+    pl.loop(done(chunks), 2 * chunks)(unit)
 
     @pl.loop(0, half)
     def _(h):
         pair(h).wait_send()
-        for copy in row(h):
-            copy.wait_send()
-        pl.when(jnp.logical_not(last))(lambda: down(h).wait_send())
-        back(h).wait_send()
+        for u in range(2):
+            for copy in row(h, u):
+                copy.wait_send()
+            pl.when(jnp.logical_not(last))(lambda: down(h, u).wait_send())
+            back(h, u).wait_send()
 
 
 def on_device(
@@ -279,7 +305,6 @@
     f32, bf16 = jnp.float32, jnp.bfloat16
     part = VMEM((half, DK, DK), f32)
     whole = VMEM((2 * half, DK, DK), f32)
-    cache = VMEM(cache_state.shape, f32)
     sems = lambda *shape: pltpu.SemaphoreType.DMA(shape)
     return pl.pallas_call(
         functools.partial(layer_kernel, A, B),
@@ -287,12 +312,12 @@
         in_specs=[smem, smem, vmem, vmem, vmem, anywhere, anywhere],
         out_specs=vmem,
         scratch_shapes=[
-            VMEM((rows, width), bf16), cache, cache, VMEM((rows, width), bf16),
+            VMEM((rows, width), bf16), VMEM((2,) + cache_state.shape, f32), VMEM((rows, width), bf16),
             VMEM((rows, width), bf16), VMEM((rows, width), f32), whole, whole,
             VMEM((rows, rows), f32), VMEM((prompts, rows, DK), bf16), VMEM((rows, DK), bf16),
             part, part, VMEM((B - 1, half, DK, DK), f32), part, part, part,
-            sems(half), sems(half), sems(B - 1, half), sems(B - 1, half),
-            sems(half), sems(half), sems(half), sems(half),
+            sems(half), sems(half), sems(B - 1, 2 * half), sems(B - 1, 2 * half),
+            sems(2 * half), sems(2 * half), sems(2 * half), sems(2 * half),
             pltpu.SemaphoreType.DMA, pltpu.SemaphoreType.DMA,
             pltpu.SemaphoreType.DMA, pltpu.SemaphoreType.DMA,
         ],

time: 34.5 us -> 36.3 us (1.052)
  Pallas kernels: 31.6 us -> 33.7 us
    pallas_call x1, Pallas kernels: 31.6 us -> 33.7 us  [on_device(): pl.pallas_call(functools.partial(layer_kernel, A, B), out_shape=jax.Shape...]
where the time goes in v1:
time: 36.3 us; the launch traced here: 36 us
  Pallas kernels  33.7 us (93%)
  local copies, waits for them, and re-layouts  2.3 us (6%)
    pallas_call x1, Pallas kernels, on_device(): pl.pallas_call(functools.partial(layer_kernel, A, B), out_shape=jax.Shape...  33.7 us
    unnamed x1, local copies, waits for them, and re-layouts  2.3 us

profile of v1, /device:TPU:29, one launch (start us, length us, event | category | flops | bytes accessed | tf_op | source)
XLA Modules:
  0.0 36.0 jit_solution(6391464400591039875)
XLA Ops:
  0.0 33.7 %layer.1 = bf16[256,2048]{1,0:T(8,128)(2,1)} custom-call(s32[4]{0:T(128)} %lengths_ref.1, s32[4]{0:T(128)} %prefix_ref.1, bf16[256,2048]{1,0:T(8,128)(2,1)} %k_ref.1, bf16[256,2048]{1,0:T(8,128)(2,1)} %v_ref.1, f32[1,2048]{1,0:T(1,128)} %bitcast.1, bf16[256,2048]{1,0:T(8,128)(2,1)} %q_hbm.1, f32[4,8,128,128]{3,2,1,0:T(8,128)} %cache_hbm.1), custom_call_target="tpu_custom_call" | custom-call | tf_op jit(solution)/shard_map/layer/pallas_call | solution.py:309
  33.7 2.3 %copy.9 = bf16[256,2048]{1,0:T(8,128)(2,1)} copy(bf16[256,2048]{1,0:T(8,128)(2,1)} %layer.1) | data formatting | bytes 2097152

commit v2 on v1

--- a/solution.py
+++ b/solution.py
@@ -46,7 +46,6 @@
     rows = k_ref.shape[0]
     prompts = cached_ref.shape[1]
     chunk_rows = DK // 2
-    chunks = 2 * half
     s = lax.axis_index("seq")
     c = lax.axis_index("inner")
     other = 1 - c
@@ -77,7 +76,7 @@
         )
 
     def piece(ref, head, u):
-        return ref.at[head, pl.ds(pl.multiple_of(u * chunk_rows, chunk_rows), chunk_rows)]
+        return ref.at[head, pl.ds(u * chunk_rows, chunk_rows)]
 
     def row(h, u):
         j = 2 * h + u
@@ -200,7 +199,7 @@
         return upper, (state - upper.astype(jnp.float32)).astype(jnp.bfloat16)
 
     def local_terms(h, side):
-        head = jnp.where(side == 0, c, other) * half + h
+        head = (other if side else c) * half + h
         cols = columns(head)
         query_feat = features(q_ref[:, cols])
         carry_query_ref[:, cols] = query_feat * carry_mask_ref[...]
@@ -231,56 +230,46 @@
         scale = 1.0 / jnp.sqrt(jnp.mean(mixed * mixed, axis=1, keepdims=True) + 1e-06)
         out_ref[:, cols] = (mixed * scale * gain_ref[:, cols]).astype(jnp.bfloat16)
 
-    def unit(i):
-        @pl.when(i < chunks)
-        def _():
-            local_terms(i // 2, i % 2)
-
-        @pl.when(i >= chunks)
-        def _():
-            h, side = (i - chunks) // 2, i % 2
-
-            @pl.when(side == 0)
-            def _():
-                back(h, 0).wait_recv()
-                back(h, 1).wait_recv()
-
-            finish(jnp.where(side == 0, c, other) * half + h)
-
-    ahead = (chunks * a) // max(A - 1, 1)
+    def both_local(h):
+        local_terms(h, 0)
+        local_terms(h, 1)
+
+    def both_finish(h):
+        back(h, 0).wait_recv()
+        back(h, 1).wait_recv()
+        finish(c * half + h)
+        finish(other * half + h)
+
+    ahead = (half * a + A // 2) // max(A - 1, 1)
     late = a >= A // 2
-
-    def done(j):
-        full = jnp.maximum(ahead, jnp.minimum(ahead + j, chunks + j - 4))
-        return jnp.where(late, full, ahead + j // 2)
-
-    pl.loop(0, ahead)(unit)
-
-    @pl.loop(0, chunks)
-    def _(j):
-        h, u = j // 2, j % 2
-        part = pl.ds(pl.multiple_of(u * chunk_rows, chunk_rows), chunk_rows)
-        for copy in row(h, u):
-            copy.wait_recv()
-        total = total_weights[0] * x_buf[h, part]
-        prefix = jnp.zeros_like(total)
-        for k in range(1, B):
-            got = row_buf[k - 1, h, part]
-            total = total + total_weights[k] * got
-            prefix = prefix + prefix_weights[k] * got
-        pl.when(jnp.logical_not(first))(lambda: down(h, u).wait_recv())
-        incoming = z_in[h, part]
-        z_out[h, part] = total + keep_row * incoming
-        pl.when(jnp.logical_not(last))(lambda: down(h, u).start())
-        at_zero = prefix + keep_prefix * incoming
-        mine, theirs = own_ref[c * half + h, part], pair_buf[h, part]
-        at_one = is_zero * mine + is_one * theirs + keep_zero * at_zero
-        back_buf[h, part] = is_one * at_zero + is_zero * at_one
-        back(h, u).start()
-        carry_ref[c * half + h, part] = is_zero * at_zero + is_one * at_one
-        pl.loop(done(j), done(j + 1))(unit)
-
-    pl.loop(done(chunks), 2 * chunks)(unit)
+    pl.loop(0, ahead)(both_local)
+
+    @pl.loop(0, half)
+    def _(h):
+        for u in range(2):
+            part = pl.ds(u * chunk_rows, chunk_rows)
+            for copy in row(h, u):
+                copy.wait_recv()
+            total = total_weights[0] * x_buf[h, part]
+            prefix = jnp.zeros_like(total)
+            for k in range(1, B):
+                got = row_buf[k - 1, h, part]
+                total = total + total_weights[k] * got
+                prefix = prefix + prefix_weights[k] * got
+            pl.when(jnp.logical_not(first))(lambda: down(h, u).wait_recv())
+            incoming = z_in[h, part]
+            z_out[h, part] = total + keep_row * incoming
+            pl.when(jnp.logical_not(last))(lambda: down(h, u).start())
+            at_zero = prefix + keep_prefix * incoming
+            mine, theirs = own_ref[c * half + h, part], pair_buf[h, part]
+            at_one = is_zero * mine + is_one * theirs + keep_zero * at_zero
+            back_buf[h, part] = is_one * at_zero + is_zero * at_one
+            back(h, u).start()
+            carry_ref[c * half + h, part] = is_zero * at_zero + is_one * at_one
+        pl.when(h >= ahead)(lambda: both_local(h))
+        pl.when(late & (h > 0))(lambda: both_finish(h - 1))
+
+    pl.loop(jnp.where(late, half - 1, 0), half)(both_finish)
 
     @pl.loop(0, half)
     def _(h):

time: 36.3 us -> 36.4 us (level)
  no operation moved by 1% of the time
where the time goes in v2:
time: 36.4 us; the launch traced here: 36.2 us
  Pallas kernels  33.9 us (93%)
  local copies, waits for them, and re-layouts  2.3 us (6%)
    pallas_call x1, Pallas kernels, on_device(): pl.pallas_call(functools.partial(layer_kernel, A, B), out_shape=jax.Shape...  33.9 us
    unnamed x1, local copies, waits for them, and re-layouts  2.3 us

profile of v2, /device:TPU:29, one launch (start us, length us, event | category | flops | bytes accessed | tf_op | source)
XLA Modules:
  0.0 36.2 jit_solution(13336915857932750964)
XLA Ops:
  0.0 33.9 %layer.1 = bf16[256,2048]{1,0:T(8,128)(2,1)} custom-call(s32[4]{0:T(128)} %lengths_ref.1, s32[4]{0:T(128)} %prefix_ref.1, bf16[256,2048]{1,0:T(8,128)(2,1)} %k_ref.1, bf16[256,2048]{1,0:T(8,128)(2,1)} %v_ref.1, f32[1,2048]{1,0:T(1,128)} %bitcast.1, bf16[256,2048]{1,0:T(8,128)(2,1)} %q_hbm.1, f32[4,8,128,128]{3,2,1,0:T(8,128)} %cache_hbm.1), custom_call_target="tpu_custom_call" | custom-call | tf_op jit(solution)/shard_map/layer/pallas_call | solution.py:298
  33.9 2.3 %copy.9 = bf16[256,2048]{1,0:T(8,128)(2,1)} copy(bf16[256,2048]{1,0:T(8,128)(2,1)} %layer.1) | data formatting | bytes 2097152

commit v3 on v2

--- a/solution.py
+++ b/solution.py
@@ -104,7 +104,12 @@
 
     near_copy = pltpu.make_async_copy(cache_hbm, cached_ref.at[0], near_sem)
     q_copy = pltpu.make_async_copy(q_hbm, q_ref, q_sem)
-    far_copy = remote(cache_hbm, cached_ref.at[1], far_s, far_r, {"inner": other})
+
+    def far(h):
+        return remote(
+            cache_hbm.at[:, h], cached_ref.at[1, :, h], far_s.at[h], far_r.at[h], {"inner": other}
+        )
+
     q_copy.start()
     near_copy.start()
 
@@ -158,16 +163,17 @@
     ends = first.astype(jnp.int32) + last.astype(jnp.int32)
     pl.semaphore_wait(barrier, B + 2 - ends)
     pair(0).start()
+    far(0).start()
     own_state(c * half)
 
     @pl.loop(1, half)
     def _(h):
         own_state(other * half + h)
         pair(h).start()
+        far(h).start()
         own_state(c * half + h)
         spread(h - 1)
 
-    far_copy.start()
     spread(half - 1)
 
     @pl.when(first)
@@ -192,7 +198,6 @@
     carry_mask_ref[...] = jnp.where(carried, 1.0, 0.0).astype(jnp.bfloat16)
     near_copy.wait()
     q_copy.wait()
-    far_copy.wait()
 
     def split(state):
         upper = state.astype(jnp.bfloat16)
@@ -231,6 +236,7 @@
         out_ref[:, cols] = (mixed * scale * gain_ref[:, cols]).astype(jnp.bfloat16)
 
     def both_local(h):
+        far(h).wait_recv()
         local_terms(h, 0)
         local_terms(h, 1)
 
@@ -274,6 +280,7 @@
     @pl.loop(0, half)
     def _(h):
         pair(h).wait_send()
+        far(h).wait_send()
         for u in range(2):
             for copy in row(h, u):
                 copy.wait_send()
@@ -307,8 +314,7 @@
             part, part, VMEM((B - 1, half, DK, DK), f32), part, part, part,
             sems(half), sems(half), sems(B - 1, 2 * half), sems(B - 1, 2 * half),
             sems(2 * half), sems(2 * half), sems(2 * half), sems(2 * half),
-            pltpu.SemaphoreType.DMA, pltpu.SemaphoreType.DMA,
-            pltpu.SemaphoreType.DMA, pltpu.SemaphoreType.DMA,
+            sems(half), sems(half), pltpu.SemaphoreType.DMA, pltpu.SemaphoreType.DMA,
         ],
         compiler_params=pltpu.CompilerParams(collective_id=0, has_side_effects=True),
         name="layer",

time: 36.4 us -> 33.4 us (0.918)
  Pallas kernels: 33.9 us -> 30.9 us
    pallas_call x1, Pallas kernels: 33.9 us -> 30.9 us  [on_device(): pl.pallas_call(functools.partial(layer_kernel, A, B), out_shape=jax.Shape...]
where the time goes in v3:
time: 33.4 us; the launch traced here: 33.2 us
  Pallas kernels  30.9 us (93%)
  local copies, waits for them, and re-layouts  2.3 us (7%)
    pallas_call x1, Pallas kernels, on_device(): pl.pallas_call(functools.partial(layer_kernel, A, B), out_shape=jax.Shape...  30.9 us
    unnamed x1, local copies, waits for them, and re-layouts  2.3 us

profile of v3, /device:TPU:29, one launch (start us, length us, event | category | flops | bytes accessed | tf_op | source)
XLA Modules:
  0.0 33.2 jit_solution(2430846636307783576)
XLA Ops:
  0.0 30.9 %layer.1 = bf16[256,2048]{1,0:T(8,128)(2,1)} custom-call(s32[4]{0:T(128)} %lengths_ref.1, s32[4]{0:T(128)} %prefix_ref.1, bf16[256,2048]{1,0:T(8,128)(2,1)} %k_ref.1, bf16[256,2048]{1,0:T(8,128)(2,1)} %v_ref.1, f32[1,2048]{1,0:T(1,128)} %bitcast.1, bf16[256,2048]{1,0:T(8,128)(2,1)} %q_hbm.1, f32[4,8,128,128]{3,2,1,0:T(8,128)} %cache_hbm.1), custom_call_target="tpu_custom_call" | custom-call | tf_op jit(solution)/shard_map/layer/pallas_call | solution.py:305
  30.9 2.3 %copy.9 = bf16[256,2048]{1,0:T(8,128)(2,1)} copy(bf16[256,2048]{1,0:T(8,128)(2,1)} %layer.1) | data formatting | bytes 2097152

commit v4 on v3

--- a/solution.py
+++ b/solution.py
@@ -272,9 +272,13 @@
             back_buf[h, part] = is_one * at_zero + is_zero * at_one
             back(h, u).start()
             carry_ref[c * half + h, part] = is_zero * at_zero + is_one * at_one
-        pl.when(h >= ahead)(lambda: both_local(h))
+        pl.when(late & (h >= ahead))(lambda: both_local(h))
+        ready = ahead + h // 2
+        early = jnp.logical_not(late) & (h % 2 == 1) & (ready < half)
+        pl.when(early)(lambda: both_local(ready))
         pl.when(late & (h > 0))(lambda: both_finish(h - 1))
 
+    pl.loop(jnp.where(late, half, jnp.minimum(ahead + half // 2, half)), half)(both_local)
     pl.loop(jnp.where(late, half - 1, 0), half)(both_finish)
 
     @pl.loop(0, half)
@@ -286,6 +290,23 @@
                 copy.wait_send()
             pl.when(jnp.logical_not(last))(lambda: down(h, u).wait_send())
             back(h, u).wait_send()
+
+
+def deliver_kernel(in_hbm, out_hbm, buffer, in_sem, out_sem):
+    pieces = in_sem.shape[0]
+    size = buffer.shape[0] // pieces
+    loads, stores = [], []
+    for i in range(pieces):
+        part = pl.ds(i * size, size)
+        loads.append(pltpu.make_async_copy(in_hbm.at[part], buffer.at[part], in_sem.at[i]))
+        stores.append(pltpu.make_async_copy(buffer.at[part], out_hbm.at[part], out_sem.at[i]))
+    for load in loads:
+        load.start()
+    for load, store in zip(loads, stores):
+        load.wait()
+        store.start()
+    for store in stores:
+        store.wait()
 
 
 def on_device(
@@ -302,7 +323,7 @@
     part = VMEM((half, DK, DK), f32)
     whole = VMEM((2 * half, DK, DK), f32)
     sems = lambda *shape: pltpu.SemaphoreType.DMA(shape)
-    return pl.pallas_call(
+    result = pl.pallas_call(
         functools.partial(layer_kernel, A, B),
         out_shape=jax.ShapeDtypeStruct((rows, width), bf16),
         in_specs=[smem, smem, vmem, vmem, vmem, anywhere, anywhere],
@@ -322,6 +343,14 @@
         new_lengths, prefix_lengths, key_vectors, value_vectors, out_gain[None, :],
         queries, cache_state,
     )
+    return pl.pallas_call(
+        deliver_kernel,
+        out_shape=jax.ShapeDtypeStruct((rows, width), bf16),
+        in_specs=[anywhere],
+        out_specs=anywhere,
+        scratch_shapes=[VMEM((rows, width), bf16), sems(4), sems(4)],
+        name="deliver",
+    )(result)
 
 
 def solution(mesh):

time: 33.4 us -> 33.1 us (level)
  local copies, waits for them, and re-layouts: 2.3 us -> 0 us
  Pallas kernels: 30.9 us -> 32.9 us
    unnamed x1 -> x0, local copies, waits for them, and re-layouts: 2.3 us -> none
    pallas_call x0 -> x1, Pallas kernels: none -> 1.98 us  [on_device(): pl.pallas_call(deliver_kernel, out_shape=jax.ShapeDtypeStruct((rows, widt...]
where the time goes in v4:
time: 33.1 us; the launch traced here: 32.9 us
  Pallas kernels  32.9 us (99%)
    pallas_call x1, Pallas kernels, on_device(): pl.pallas_call(functools.partial(layer_kernel, A, B), out_shape=jax.Shape...  30.9 us
    pallas_call x1, Pallas kernels, on_device(): pl.pallas_call(deliver_kernel, out_shape=jax.ShapeDtypeStruct((rows, widt...  1.98 us

profile of v4, /device:TPU:29, one launch (start us, length us, event | category | flops | bytes accessed | tf_op | source)
XLA Modules:
  0.0 32.9 jit_solution(10719288502688681636)
XLA Ops:
  0.0 30.9 %layer.1.in_hbm = bf16[256,2048]{1,0:T(8,128)(2,1)} custom-call(s32[4]{0:T(128)} %lengths_ref.1, s32[4]{0:T(128)} %prefix_ref.1, bf16[256,2048]{1,0:T(8,128)(2,1)} %k_ref.1, bf16[256,2048]{1,0:T(8,128)(2,1)} %v_ref.1, f32[1,2048]{1,0:T(1,128)} %bitcast.1, bf16[256,2048]{1,0:T(8,128)(2,1)} %q_hbm.1, f32[4,8,128,128]{3,2,1,0:T(8,128)} %cache_hbm.1), custom_call_target="tpu_custom_call" | custom-call | tf_op jit(solution)/shard_map/layer/pallas_call | solution.py:326
  31.0 2.0 %deliver.1 = bf16[256,2048]{1,0:T(8,128)(2,1)} custom-call(bf16[256,2048]{1,0:T(8,128)(2,1)} %layer.1.in_hbm), custom_call_target="tpu_custom_call" | custom-call | tf_op jit(solution)/shard_map/deliver/pallas_call | solution.py:346

commit v5 on v4

--- a/solution.py
+++ b/solution.py
@@ -45,7 +45,7 @@
     half = pair_buf.shape[0]
     rows = k_ref.shape[0]
     prompts = cached_ref.shape[1]
-    chunk_rows = DK // 2
+    chunk_rows = DK // 4
     s = lax.axis_index("seq")
     c = lax.axis_index("inner")
     other = 1 - c
@@ -79,7 +79,7 @@
         return ref.at[head, pl.ds(u * chunk_rows, chunk_rows)]
 
     def row(h, u):
-        j = 2 * h + u
+        j = 4 * h + u
         return [
             remote(
                 piece(x_buf, h, u), piece(row_buf.at[k], h, u), row_s.at[k, j], row_r.at[k, j],
@@ -89,14 +89,14 @@
         ]
 
     def down(h, u):
-        j = 2 * h + u
+        j = 4 * h + u
         return remote(
             piece(z_out, h, u), piece(z_in, h, u), z_s.at[j], z_r.at[j],
             {"seq": jnp.minimum(s + B, A * B - 1)},
         )
 
     def back(h, u):
-        j = 2 * h + u
+        j = 4 * h + u
         return remote(
             piece(back_buf, h, u), piece(carry_ref, c * half + h, u), back_s.at[j], back_r.at[j],
             {"inner": other},
@@ -155,7 +155,7 @@
     def spread(h):
         pair(h).wait_recv()
         x_buf[h] = mine_weight * own_ref[c * half + h] + theirs_weight * pair_buf[h]
-        for u in range(2):
+        for u in range(4):
             for copy in row(h, u):
                 copy.start()
 
@@ -241,8 +241,8 @@
         local_terms(h, 1)
 
     def both_finish(h):
-        back(h, 0).wait_recv()
-        back(h, 1).wait_recv()
+        for u in range(4):
+            back(h, u).wait_recv()
         finish(c * half + h)
         finish(other * half + h)
 
@@ -252,7 +252,7 @@
 
     @pl.loop(0, half)
     def _(h):
-        for u in range(2):
+        for u in range(4):
             part = pl.ds(u * chunk_rows, chunk_rows)
             for copy in row(h, u):
                 copy.wait_recv()
@@ -285,7 +285,7 @@
     def _(h):
         pair(h).wait_send()
         far(h).wait_send()
-        for u in range(2):
+        for u in range(4):
             for copy in row(h, u):
                 copy.wait_send()
             pl.when(jnp.logical_not(last))(lambda: down(h, u).wait_send())
@@ -333,8 +333,8 @@
             VMEM((rows, width), bf16), VMEM((rows, width), f32), whole, whole,
             VMEM((rows, rows), f32), VMEM((prompts, rows, DK), bf16), VMEM((rows, DK), bf16),
             part, part, VMEM((B - 1, half, DK, DK), f32), part, part, part,
-            sems(half), sems(half), sems(B - 1, 2 * half), sems(B - 1, 2 * half),
-            sems(2 * half), sems(2 * half), sems(2 * half), sems(2 * half),
+            sems(half), sems(half), sems(B - 1, 4 * half), sems(B - 1, 4 * half),
+            sems(4 * half), sems(4 * half), sems(4 * half), sems(4 * half),
             sems(half), sems(half), pltpu.SemaphoreType.DMA, pltpu.SemaphoreType.DMA,
         ],
         compiler_params=pltpu.CompilerParams(collective_id=0, has_side_effects=True),

time: 33.1 us -> 33.9 us (1.024)
  Pallas kernels: 32.9 us -> 33.7 us
    pallas_call x1, Pallas kernels: 30.9 us -> 31.7 us  [on_device(): pl.pallas_call(functools.partial(layer_kernel, A, B), out_shape=jax.Shape...]
where the time goes in v5:
time: 33.9 us; the launch traced here: 33.7 us
  Pallas kernels  33.7 us (99%)
    pallas_call x1, Pallas kernels, on_device(): pl.pallas_call(functools.partial(layer_kernel, A, B), out_shape=jax.Shape...  31.7 us
    pallas_call x1, Pallas kernels, on_device(): pl.pallas_call(deliver_kernel, out_shape=jax.ShapeDtypeStruct((rows, widt...  1.98 us

profile of v5, /device:TPU:29, one launch (start us, length us, event | category | flops | bytes accessed | tf_op | source)
XLA Modules:
  0.0 33.7 jit_solution(2542019500549415481)
XLA Ops:
  0.0 31.7 %layer.1.in_hbm = bf16[256,2048]{1,0:T(8,128)(2,1)} custom-call(s32[4]{0:T(128)} %lengths_ref.1, s32[4]{0:T(128)} %prefix_ref.1, bf16[256,2048]{1,0:T(8,128)(2,1)} %k_ref.1, bf16[256,2048]{1,0:T(8,128)(2,1)} %v_ref.1, f32[1,2048]{1,0:T(1,128)} %bitcast.1, bf16[256,2048]{1,0:T(8,128)(2,1)} %q_hbm.1, f32[4,8,128,128]{3,2,1,0:T(8,128)} %cache_hbm.1), custom_call_target="tpu_custom_call" | custom-call | tf_op jit(solution)/shard_map/layer/pallas_call | solution.py:326
  31.8 2.0 %deliver.1 = bf16[256,2048]{1,0:T(8,128)(2,1)} custom-call(bf16[256,2048]{1,0:T(8,128)(2,1)} %layer.1.in_hbm), custom_call_target="tpu_custom_call" | custom-call | tf_op jit(solution)/shard_map/deliver/pallas_call | solution.py:346
